TPU v7x, 32 devices: a whole 2x2x4 slice. The times are simulated.
32 devices in a mesh: gx: 8 (over z, y), gy: 4 (over x, core).
Axes of the slice: x: 2, y: 2, z: 4, core: 2. Of those that a mesh axis runs over, the one named last changes fastest.
Arguments:
- psi: float32 [2, 256, 16, 1024], P(None, 'gx', None, 'gy'), may hold values from -6 to 6
- potential: float32 [256, 16, 1024], P('gx', None, 'gy'), may hold values from 0 to 4
Outputs:
- psi_half: float32 [2, 256, 16, 1024], P(None, 'gx', None, 'gy')
All inputs are finite; a program needn't handle non-finite values.
Results may differ from a plain program's by a relative error of at most 0.00005.
Values sent between devices are 32-bit elements; how exact they have to be, the bound alone decides.
A program may use at most 64 MiB of HBM per device.

v0:
```python
import jax
import jax.numpy as jnp
import numpy as np
from jax import lax
from jax.sharding import PartitionSpec as P

RYZ = 2


def with_halo(value, sides, width):
    for axis, dim in sides:
        peers, length = (lax.axis_size(axis), value.shape[dim])
        up = [(i, (i + 1) % peers) for i in range(peers - 1)]
        down = [(j, i) for i, j in up]
        last = lax.slice_in_dim(value, length - width, length, axis=dim)
        first = lax.slice_in_dim(value, 0, width, axis=dim)
        before = lax.ppermute(last, axis, up)
        after = lax.ppermute(first, axis, down)
        value = jnp.concatenate([before, value, after], axis=dim)
    return value


def cmul(left, right):
    return jnp.stack(
        [left[0] * right[0] - left[1] * right[1], left[0] * right[1] + left[1] * right[0]]
    )


def cinv(value):
    denom = value[0] * value[0] + value[1] * value[1]
    return jnp.stack([value[0] / denom, -value[1] / denom])


def local_inverse(cells):
    coef = 256.0 * cells * cells
    identity = np.eye(cells)
    cp_re_list = []
    cp_im_list = []
    dp_re_list = []
    dp_im_list = []
    cp_re = 0.0
    cp_im = 0.0
    dp_re = np.zeros(cells)
    dp_im = np.zeros(cells)
    for index in range(cells):
        piv_re = 1.0 - coef * cp_im
        piv_im = 2.0 * coef + coef * cp_re
        denom = piv_re * piv_re + piv_im * piv_im
        cp_re = -coef * piv_im / denom
        cp_im = -coef * piv_re / denom
        num_re = identity[index] - coef * dp_im
        num_im = coef * dp_re
        dp_re = (num_re * piv_re + num_im * piv_im) / denom
        dp_im = (num_im * piv_re - num_re * piv_im) / denom
        cp_re_list.append(cp_re)
        cp_im_list.append(cp_im)
        dp_re_list.append(dp_re)
        dp_im_list.append(dp_im)
    inv_re = np.zeros((cells, cells))
    inv_im = np.zeros((cells, cells))
    later_re = np.zeros(cells)
    later_im = np.zeros(cells)
    for index in range(cells - 1, -1, -1):
        next_re = dp_re_list[index] - (cp_re_list[index] * later_re - cp_im_list[index] * later_im)
        next_im = dp_im_list[index] - (cp_re_list[index] * later_im + cp_im_list[index] * later_re)
        later_re, later_im = (next_re, next_im)
        inv_re[index] = later_re
        inv_im[index] = later_im
    return (inv_re, inv_im, coef)


def shards(psi, potential):
    cells = psi.shape[1]
    count = lax.axis_size("gx")
    place = lax.axis_index("gx")
    inv_re, inv_im, coef = local_inverse(cells)
    upper_half = np.concatenate([inv_re, -inv_im], axis=1)
    lower_half = np.concatenate([inv_im, inv_re], axis=1)
    big = np.concatenate([upper_half, lower_half], axis=0).astype(np.float32)
    g_vec = jnp.asarray(np.stack([-coef * inv_im[:, 0], coef * inv_re[:, 0]]).astype(np.float32))
    h_vec = jnp.asarray(
        np.stack([-coef * inv_im[:, cells - 1], coef * inv_re[:, cells - 1]]).astype(np.float32)
    )
    s_val = g_vec[:, 0]
    t_val = g_vec[:, cells - 1]
    real_part, imag_part = (psi[0], psi[1])
    theta = 0.5 * (potential + real_part * real_part + imag_part * imag_part)
    cosine, sine = (jnp.cos(theta), jnp.sin(theta))
    turned = jnp.stack(
        [real_part * cosine + imag_part * sine, imag_part * cosine - real_part * sine]
    )
    padded = with_halo(turned, (("gy", 3),), 1)
    lap_y = padded[:, :, :, 2:] + padded[:, :, :, :-2] - 2.0 * turned
    z_padded = jnp.pad(turned, ((0, 0), (0, 0), (1, 1), (0, 0)))
    lap_z = z_padded[:, :, 2:] + z_padded[:, :, :-2] - 2.0 * turned
    side = RYZ * (lap_y + lap_z)
    rhs = jnp.stack([2.0 * turned[0] - side[1], 2.0 * turned[1] + side[0]])
    planes = rhs.shape[2]
    lines = rhs.shape[3]
    flat = rhs.reshape(2 * cells, planes * lines)
    local = jnp.dot(jnp.asarray(big), flat, precision=lax.Precision.HIGHEST).reshape(
        2, cells, planes, lines
    )
    first_val = local[:, 0]
    last_val = local[:, cells - 1]

    def advance(alpha, unused):
        q_val = cinv(
            jnp.stack(
                [
                    1.0 - (s_val[0] * alpha[0] - s_val[1] * alpha[1]),
                    -(s_val[0] * alpha[1] + s_val[1] * alpha[0]),
                ]
            )
        )
        aq_val = cmul(alpha, q_val)
        c_val = cmul(t_val, jnp.stack([1.0, 0.0]) + cmul(aq_val, s_val))
        mu_val = cmul(q_val, t_val)
        new_alpha = s_val + cmul(cmul(t_val, t_val), aq_val)
        return (new_alpha, (alpha, q_val, c_val, mu_val))

    unused, tables = lax.scan(advance, jnp.zeros((2,), jnp.float32), None, length=count)
    alphas, q_vals, c_vals, mu_vals = tables
    alpha_here = lax.dynamic_index_in_dim(alphas, place, 0, keepdims=False)
    q_here = lax.dynamic_index_in_dim(q_vals, place, 0, keepdims=False)
    mu_here = lax.dynamic_index_in_dim(mu_vals, place, 0, keepdims=False)
    fwd_term = last_val + cmul(cmul(t_val, cmul(alpha_here, q_here)), first_val)
    positions = jnp.arange(count, dtype=jnp.int32)

    def fwd_row(row, item):
        factor, index = item
        onehot = jnp.stack(
            [(positions == index).astype(jnp.float32), jnp.zeros((count,), jnp.float32)]
        )
        return (cmul(factor, row) + onehot, row)

    unused, fwd_rows = lax.scan(fwd_row, jnp.zeros((2, count), jnp.float32), (c_vals, positions))
    fwd_weights = lax.dynamic_index_in_dim(fwd_rows, place, 0, keepdims=False)
    piece = lax.all_gather(fwd_term[None], "gx", axis=0, tiled=True)
    weights = lax.slice_in_dim(fwd_weights, 0, piece.shape[0], axis=1)
    part_re = jnp.einsum(
        "k,kzy->zy", weights[0], piece[:, 0], precision=lax.Precision.HIGHEST
    ) - jnp.einsum("k,kzy->zy", weights[1], piece[:, 1], precision=lax.Precision.HIGHEST)
    part_im = jnp.einsum(
        "k,kzy->zy", weights[0], piece[:, 1], precision=lax.Precision.HIGHEST
    ) + jnp.einsum("k,kzy->zy", weights[1], piece[:, 0], precision=lax.Precision.HIGHEST)
    beta_prev = jnp.zeros_like(fwd_term) + jnp.stack([part_re, part_im])
    nu_here = cmul(q_here, first_val + cmul(s_val, beta_prev))

    def back_row(row, item):
        factor, index = item
        onehot = jnp.stack(
            [(positions == index).astype(jnp.float32), jnp.zeros((count,), jnp.float32)]
        )
        return (cmul(factor, row) + onehot, row)

    unused, back_rows = lax.scan(
        back_row, jnp.zeros((2, count), jnp.float32), (mu_vals, positions), reverse=True
    )
    back_weights = lax.dynamic_index_in_dim(back_rows, place, 0, keepdims=False)
    piece = lax.all_gather(nu_here[None], "gx", axis=0, tiled=True)
    weights = lax.slice_in_dim(back_weights, 0, piece.shape[0], axis=1)
    part_re = jnp.einsum(
        "k,kzy->zy", weights[0], piece[:, 0], precision=lax.Precision.HIGHEST
    ) - jnp.einsum("k,kzy->zy", weights[1], piece[:, 1], precision=lax.Precision.HIGHEST)
    part_im = jnp.einsum(
        "k,kzy->zy", weights[0], piece[:, 1], precision=lax.Precision.HIGHEST
    ) + jnp.einsum("k,kzy->zy", weights[1], piece[:, 0], precision=lax.Precision.HIGHEST)
    next_first = jnp.zeros_like(nu_here) + jnp.stack([part_re, part_im])
    first_here = cmul(mu_here, next_first) + nu_here
    edge_prev = cmul(alpha_here, first_here) + beta_prev
    from_left = cmul(g_vec[:, :, None, None], edge_prev[:, None])
    from_right = cmul(h_vec[:, :, None, None], next_first[:, None])
    return local + from_left + from_right - turned


def solution(mesh):
    return jax.shard_map(
        shards,
        mesh=mesh,
        in_specs=(P(None, "gx", None, "gy"), P("gx", None, "gy")),
        out_specs=P(None, "gx", None, "gy"),
        check_vma=False,
    )
```

profile of v0, /device:TPU:0, one launch (start us, length us, event | category | flops | bytes accessed | tf_op | source)
XLA Modules:
  0.0 309.6 jit_solution(17856614827695865240)
XLA Ops:
  0.0 3.6 %fusion.18 = (f32[32,16,256]{2,1,0:T(8,128)S(1)}, f32[32,16,256]{2,1,0:T(8,128)S(1)}) fusion(f32[2,32,16,256]{3,2,1,0:T(8,128)} %param.11, f32[32,16,256]{2,1,0:T(8,128)} %param.12), kind=kLoop, calls=%fused_computation.56 | loop fusion | flops 1441792 | bytes 2621440 | tf_op jit(solution)/shard_map/add | solution.py:90
  3.9 1.3 collective-permute-start
  5.2 3.8 %collective-permute-start.1 = (f32[2,32,16,1]{3,2,1,0:T(8,128)S(1)}, f32[2,32,16,1]{3,2,1,0:T(8,128)}, u32[]{:S(2)}, u32[]{:S(2)}) collective-permute-start(f32[2,32,16,1]{3,2,1,0:T(8,128)S(1)} %get-tuple-element.456), channel_id=1, source_target_pairs={{0,1},{1,2},{2,3},{4,5},{5,6},{6,7},{8,9},{9,10},{10,11},{12,13},{... | collective-permute-start | bytes 12296 | tf_op jit(solution)/shard_map/ppermute | solution.py:17
  9.7 162.3 %while.56 = (s32[]{:T(128)}, f32[2]{0:T(128)S(1)}, f32[8,2]{1,0:T(8,128)S(1)}, f32[8,2]{1,0:T(8,128)S(1)}, f32[8,2]{1,0:T(8,128)S(1)}, /*index=5*/f32[8,2]{1,0:T...) while((s32[]{:T(128)}, f32[2]{0:T(128)S(1)}, ...), condition=%wide.region_1.2_spmd.clone.clone, body=%wide.region_0.1_spmd.clone.clone.sunk | while | flops 63 | bytes 928 | solution.py:122
  173.8 26.4 %while.55 = (s32[]{:T(128)}, f32[2,8]{1,0:T(2,128)S(1)}, f32[8,2,8]{2,1,0:T(2,128)S(1)}, f32[8,2]{1,0:T(8,128)S(1)}, s32[8]{0:T(128)S(1)}, /*index=5*/s32[]{:T(128)}, s32[]{:T(128)}) while((s32[]{:T(128)}, f32[2,8]{1,0:T(2,128)S(1)}, f32[8,2,8]{2,1,0:T(2,128)S(1)}, f32[8,2]{1,0:T(8,128)S(1)}, s32[8]{0:T(128)S(1)}, ...), condition=%wide.region_5.6_spmd.clone.clone, body=%wide.region_4.5_spmd.clone.clone.sunk | while | flops 123 | bytes 3535 | solution.py:137
  175.8 1.3 multiply_subtract_fusion.10
  177.8 0.7 compare_bitcast_fusion.5
  179.1 1.3 multiply_subtract_fusion.10
  182.4 1.3 multiply_subtract_fusion.10
  185.7 1.3 multiply_subtract_fusion.10
  189.0 1.3 multiply_subtract_fusion.10
  192.3 1.3 multiply_subtract_fusion.10
  195.7 1.3 multiply_subtract_fusion.10
  199.0 1.3 multiply_subtract_fusion.10
  200.3 26.6 %while.54 = (s32[]{:T(128)}, f32[2,8]{1,0:T(2,128)S(1)}, f32[8,2,8]{2,1,0:T(2,128)S(1)}, f32[8,2]{1,0:T(8,128)S(1)}, s32[8]{0:T(128)S(1)}, /*index=5*/s32[]{:T(128)}, s32[]{:T(128)}, s32[]{:T(128)}) while((s32[]{:T(128)}, f32[2,8]{1,0:T(2,128)S(1)}, f32[8,2,8]{2,1,0:T(2,128)S(1)}, f32[8,2]{1,0:T(8,128)S(1)}, ...), condition=%wide.region_3.4_spmd.clone.clone, body=%wide.region_2.3_spmd.clone.clone.sunk | while | flops 124 | bytes 3555 | solution.py:157
  202.3 1.3 multiply_subtract_fusion.9
  205.6 1.3 multiply_subtract_fusion.9
  208.9 1.3 multiply_subtract_fusion.9
  212.2 1.3 multiply_subtract_fusion.9
  215.6 1.3 multiply_subtract_fusion.9
  218.9 1.3 multiply_subtract_fusion.9
  222.2 1.3 multiply_subtract_fusion.9
  225.5 1.3 multiply_subtract_fusion.9
  232.1 1.9 fusion.5
  235.1 1.0 fusion.68
  236.5 32.7 %all_gather.6 = f32[8,2,16,256]{3,2,1,0:T(8,128)S(1)} all-gather(f32[1,2,16,256]{3,2,1,0:T(8,128)S(1)} %fusion.37), channel_id=1, replica_groups=mesh['gx'=8,'gy'=4] {'gx'}, dimensions={0}, use_global_device_ids=true | all-gather | bytes 294912 | tf_op jit(solution)/shard_map/all_gather | solution.py:139
  270.6 1.3 multiply_subtract_fusion.5
  271.9 30.7 %all-gather = f32[16,16,256]{2,1,0:T(8,128)S(1)} all-gather(f32[2,16,256]{2,1,0:T(8,128)S(1)} %pad_maximum_fusion.6), channel_id=2, replica_groups=mesh['gx'=8,'gy'=4] {'gx'}, dimensions={0}, use_global_device_ids=true | all-gather | bytes 294912 | tf_op jit(solution)/shard_map/all_gather | solution.py:161
  303.9 1.2 subtract_bitcast_fusion
  305.1 1.2 add_bitcast_fusion
  306.4 1.4 multiply_subtract_fusion.4
  308.2 1.5 fusion.9
  (269 shorter events, 56.4 us)
Async XLA Ops:
  3.9 228.2 %collective-permute-start = (f32[2,32,16,1]{3,2,1,0:T(8,128)S(1)}, f32[2,32,16,1]{3,2,1,0:T(8,128)}, u32[]{:S(2)}, u32[]{:S(2)}) collective-permute-start(f32[2,32,16,1]{3,2,1,0:T(8,128)S(1)} %get-tuple-element.455), channel_id=1, source_target_pairs={{1,0},{2,1},{3,2},{5,4},{6,5},{7,6},{9,8},{10,9},{11,10},{13,12},{... | collective-permute-start | bytes 12296 | tf_op jit(solution)/shard_map/ppermute | solution.py:18
  5.2 226.9 %collective-permute-start.1 = (f32[2,32,16,1]{3,2,1,0:T(8,128)S(1)}, f32[2,32,16,1]{3,2,1,0:T(8,128)}, u32[]{:S(2)}, u32[]{:S(2)}) collective-permute-start(f32[2,32,16,1]{3,2,1,0:T(8,128)S(1)} %get-tuple-element.456), channel_id=1, source_target_pairs={{0,1},{1,2},{2,3},{4,5},{5,6},{6,7},{8,9},{9,10},{10,11},{12,13},{... | collective-permute-start | bytes 12296 | tf_op jit(solution)/shard_map/ppermute | solution.py:17
  9.0 0.7 copy-start
  9.0 0.7 copy-start.1
  9.0 0.7 copy-start.3
  234.4 0.8 copy-start.2
  270.6 37.2 %copy-start.6 = (f32[32]{0:T(128)S(1)}, f32[32]{0:T(128)}, u32[]{:S(2)}) copy-start(f32[32]{0:T(128)} %constant.154) | copy-start | bytes 388
  270.6 37.2 %copy-start.7 = (f32[32]{0:T(128)S(1)}, f32[32]{0:T(128)}, u32[]{:S(2)}) copy-start(f32[32]{0:T(128)} %constant.152) | copy-start | bytes 388
  302.9 5.0 %copy-start.4 = (f32[32]{0:T(128)S(1)}, f32[32]{0:T(128)}, u32[]{:S(2)}) copy-start(f32[32]{0:T(128)} %constant.150) | copy-start | bytes 388
  303.0 5.0 %copy-start.5 = (f32[32]{0:T(128)S(1)}, f32[32]{0:T(128)}, u32[]{:S(2)}) copy-start(f32[32]{0:T(128)} %constant.131) | copy-start | bytes 388
where the time goes:
time: 313 us; the launch traced here: 310 us
  loops' own time  144 us (46%)
  blocking collectives  63.5 us (20%)
  other arithmetic  47.9 us (15%)
  local copies, waits for them, and re-layouts  39.6 us (13%)
  between operations  5.62 us (2%)
  starting transfers between devices  5.13 us (2%)
  matrix products  3.47 us (1%)
    another operation x1, loops' own time, shards(): lax.scan(advance, jnp.zeros((2,), jnp.float32), None, length=count)  144 us
    all_gather x1, blocking collectives, shards(): piece = lax.all_gather(fwd_term[None], 'gx', axis=0, tiled=True)  32.7 us
    all_gather x1, blocking collectives, shards(): piece = lax.all_gather(nu_here[None], 'gx', axis=0, tiled=True)  30.7 us
    sub x21, other arithmetic, cmul(): left[0] * right[0] - left[1] * right[1]  23.7 us
    slice x18, local copies, waits for them, and re-layouts, cmul(): left[0] * right[0] - left[1] * right[1]  11.3 us
    dynamic_slice x32, local copies, waits for them, and re-layouts, shards(): lax.scan(fwd_row, jnp.zeros((2, count), jnp.float32), (c_vals, positions))  10.4 us
  transfers between devices with their start and end apart: 2, of which 0 were waited for; matrix products, arithmetic and copies ran while one was open for 23% of the time, Pallas kernels for 0%

commit v1 on v0

v1 whole, which is shorter than its diff:
```python
import functools

import jax
import jax.numpy as jnp
import numpy as np
from jax import lax
from jax.experimental import pallas as pl
from jax.experimental.pallas import tpu as pltpu
from jax.sharding import PartitionSpec as P

RYZ = 2.0
LANES = 128
MESH = pl.DeviceIdType.MESH


def tables(cells, count):
    coef = 256.0 * cells * cells
    total = cells * count
    lam = np.arccosh(np.complex128(1.0 - 0.5j / coef))
    sh = lambda m: np.sinh(lam * m)
    scale = -(1j / coef) / (sh(1) * sh(total + 1))
    x0 = cells * np.arange(count, dtype=np.float64)
    end = x0 + cells
    f_q = sh(end) - sh(end + 1)
    f_e = sh(end + 1)
    r_q = sh(total + 1 - end) - sh(total - end)
    r_e = sh(total - end)
    w_l = scale * sh(total + 1 - x0)
    w_r = scale * sh(x0)
    d_l = scale * (sh(total - x0) - sh(total + 1 - x0))
    d_r = scale * (sh(x0 + 1) - sh(x0))
    rows = [f_q, f_e, r_q, r_e, w_l, w_r, d_l, d_r]
    place = np.stack([part for row in rows for part in (row.real, row.imag)], axis=1)
    m = np.arange(1, cells + 1, dtype=np.float64)
    g1 = sh(cells + 1 - m) / sh(1)
    ge = g1 - sh(cells - m) / sh(1)
    weights = np.zeros((8, LANES))
    for row, value in enumerate([g1.real, g1.imag, ge.real, ge.imag]):
        weights[row, :cells] = value
    return place.astype(np.float32).reshape(-1), weights.astype(np.float32), coef


def sincos(theta):
    n = jnp.floor(theta * np.float32(2.0 / np.pi) + 0.5)
    r = theta - n * np.float32(1.5703125)
    r = r - n * np.float32(4.837512969970703125e-4)
    r = r - n * np.float32(7.549789954891882e-8)
    r2 = r * r
    s = r2 * np.float32(-1.9515295891e-4) + np.float32(8.3321608736e-3)
    s = s * r2 + np.float32(-1.6666654611e-1)
    s = s * (r2 * r) + r
    c = r2 * np.float32(2.443315711809948e-5) + np.float32(-1.388731625493765e-3)
    c = c * r2 + np.float32(4.166664568298827e-2)
    c = c * (r2 * r2) + (1.0 - 0.5 * r2)
    q = n.astype(jnp.int32)
    odd = (q & 1) == 1
    sine = jnp.where(odd, c, s)
    cosine = jnp.where(odd, s, c)
    sine = jnp.where((q & 2) == 2, -sine, sine)
    cosine = jnp.where(((q + 1) & 2) == 2, -cosine, cosine)
    return sine, cosine


def turn(re, im, pot):
    theta = 0.5 * (pot + re * re + im * im)
    sine, cosine = sincos(theta)
    return re * cosine + im * sine, im * cosine - re * sine


def kernel(count, wide, coef, chunk, psi, pot, place_ref, weights, out, psi_v, pot_v, turned, rho,
           out_v, edge, halo, fr, recv, in_sem, out_sem, hs_sem, hr_sem, s_sem, r_sem):
    cells, planes, lines = pot_v.shape
    chunks = cells // chunk
    gx = lax.axis_index("gx")
    gy = lax.axis_index("gy")
    inv = np.float32(1.0 / coef)

    def load(i):
        part = pl.ds(i * chunk, chunk)
        return (
            pltpu.make_async_copy(psi.at[:, part], psi_v.at[:, part], in_sem.at[0, i]),
            pltpu.make_async_copy(pot.at[part], pot_v.at[part], in_sem.at[1, i]),
        )

    for i in range(chunks):
        for copy in load(i):
            copy.start()

    barrier = pltpu.get_barrier_semaphore()

    @pl.loop(1, count)
    def _(off):
        pl.semaphore_signal(barrier, inc=1, device_id={"gx": lax.rem(gx + off, count)},
                            device_id_type=MESH)

    @pl.when(gy > 0)
    def _():
        pl.semaphore_signal(barrier, inc=1, device_id={"gy": gy - 1}, device_id_type=MESH)

    @pl.when(gy < wide - 1)
    def _():
        pl.semaphore_signal(barrier, inc=1, device_id={"gy": gy + 1}, device_id_type=MESH)

    lane = lax.broadcasted_iota(jnp.int32, (planes, LANES), 1)
    for i in range(chunks):
        for copy in load(i):
            copy.wait()

    def pack(c, acc):
        new = []
        for which in range(3):
            src = (psi_v.at[0, c], psi_v.at[1, c], pot_v.at[c])[which]
            first = src[:, 0:LANES][:, 0:1]
            last = src[:, lines - LANES : lines][:, LANES - 1 : LANES]
            new.append(jnp.where(lane == c, first, acc[2 * which]))
            new.append(jnp.where(lane == c, last, acc[2 * which + 1]))
        return tuple(new)

    zero_edge = jnp.zeros((planes, LANES), jnp.float32)
    packed = lax.fori_loop(0, cells, pack, (zero_edge,) * 6, unroll=4)
    for which in range(3):
        edge[0, which] = packed[2 * which]
        edge[1, which] = packed[2 * which + 1]

    greeted = jnp.where(gy > 0, 1, 0) + jnp.where(gy < wide - 1, 1, 0)
    pl.semaphore_wait(barrier, count - 1 + greeted)

    down = pltpu.make_async_remote_copy(edge.at[0], halo.at[1], hs_sem.at[0], hr_sem.at[1],
                                        device_id={"gy": gy - 1}, device_id_type=MESH)
    up = pltpu.make_async_remote_copy(edge.at[1], halo.at[0], hs_sem.at[1], hr_sem.at[0],
                                      device_id={"gy": gy + 1}, device_id_type=MESH)

    @pl.when(gy > 0)
    def _():
        down.start()

    @pl.when(gy == 0)
    def _():
        halo[0] = jnp.zeros(halo.shape[1:], jnp.float32)

    @pl.when(gy < wide - 1)
    def _():
        up.start()

    @pl.when(gy == wide - 1)
    def _():
        halo[1] = jnp.zeros(halo.shape[1:], jnp.float32)

    def advance(c, carry):
        e_re, e_im, q_re, q_im = carry
        t_re, t_im = turn(psi_v[0, c], psi_v[1, c], pot_v[c])
        turned[0, c] = t_re
        turned[1, c] = t_im
        e_re = e_re + (t_re + inv * q_im)
        e_im = e_im + (t_im - inv * q_re)
        return e_re, e_im, q_re + e_re, q_im + e_im

    zero = jnp.zeros((planes, lines), jnp.float32)
    e_re, e_im, q_re, q_im = lax.fori_loop(0, cells, advance, (zero,) * 4, unroll=2)

    @pl.when(gy > 0)
    def _():
        up.wait_recv()

    @pl.when(gy < wide - 1)
    def _():
        down.wait_recv()

    sides = []
    sums = []
    for side in range(2):
        h_re, h_im = turn(halo[side, 0], halo[side, 1], halo[side, 2])
        sides.append((h_re, h_im))
        g_re, g_im = weights[0:1, :], weights[1:2, :]
        k_re, k_im = weights[2:3, :], weights[3:4, :]
        total = lambda x: jnp.sum(x, axis=1, keepdims=True)
        sums.append((
            (total(k_re * h_re - k_im * h_im), total(k_re * h_im + k_im * h_re)),
            (total(g_re * h_re - g_im * h_im), total(g_re * h_im + g_im * h_re)),
        ))

    col = lax.broadcasted_iota(jnp.int32, (planes, lines), 1)
    row = lax.broadcasted_iota(jnp.int32, (planes, lines), 0)
    at_first, at_last = col == 0, col == lines - 1
    at_bottom, at_top = row == 0, row == planes - 1

    def lap(x, first, last):
        left = jnp.where(at_first, first, pltpu.roll(x, 1, 1))
        right = jnp.where(at_last, last, pltpu.roll(x, lines - 1, 1))
        below = jnp.where(at_bottom, 0.0, pltpu.roll(x, 1, 0))
        above = jnp.where(at_top, 0.0, pltpu.roll(x, planes - 1, 0))
        return ((left + right) + (below + above)) - 4.0 * x

    def stencil(re, im, first, last):
        lap_re = lap(re, first[0], last[0])
        lap_im = lap(im, first[1], last[1])
        return 2.0 * re - RYZ * lap_im, 2.0 * im + RYZ * lap_re

    e_re, e_im = stencil(e_re, e_im, sums[0][0], sums[1][0])
    q_re, q_im = stencil(q_re, q_im, sums[0][1], sums[1][1])

    def scalar(index):
        return place_ref[gx * 16 + 2 * index], place_ref[gx * 16 + 2 * index + 1]

    def both(a, x, b, y):
        return (
            (a[0] * x[0] - a[1] * x[1]) + (b[0] * y[0] - b[1] * y[1]),
            (a[0] * x[1] + a[1] * x[0]) + (b[0] * y[1] + b[1] * y[0]),
        )

    for which in range(2):
        value = both(scalar(2 * which), (q_re, q_im), scalar(2 * which + 1), (e_re, e_im))
        fr[which, 0] = value[0]
        fr[which, 1] = value[1]

    def message(peer):
        return pltpu.make_async_remote_copy(
            fr.at[jnp.where(peer < gx, 1, 0)], recv.at[gx], s_sem.at[peer], r_sem.at[gx],
            device_id={"gx": peer}, device_id_type=MESH)

    @pl.loop(1, count)
    def _(off):
        message(lax.rem(gx + off, count)).start()

    h_all = (sides[0][0], sides[0][1], sides[1][0], sides[1][1])

    def fill(c, h):
        first = (h[0][:, 0:1], h[1][:, 0:1])
        last = (h[2][:, 0:1], h[3][:, 0:1])
        r_re, r_im = stencil(turned[0, c], turned[1, c], first, last)
        rho[0, c] = -inv * r_im
        rho[1, c] = inv * r_re
        return tuple(pltpu.roll(x, LANES - 1, 1) for x in h)

    lax.fori_loop(0, cells, fill, h_all, unroll=2)

    def arrival(k):
        return pltpu.make_async_remote_copy(
            fr.at[0], recv.at[k], s_sem.at[k], r_sem.at[k],
            device_id={"gx": k}, device_id_type=MESH)

    def take(k, acc):
        arrival(k).wait_recv()
        return acc[0] + recv[k, 0], acc[1] + recv[k, 1]

    left = lax.fori_loop(0, gx, take, (zero, zero))
    right = lax.fori_loop(gx + 1, count, take, (fr[1, 0], fr[1, 1]))
    w = both(scalar(4), left, scalar(5), right)
    d = both(scalar(6), left, scalar(7), right)

    def store(i):
        part = pl.ds(i * chunk, chunk)
        return pltpu.make_async_copy(out_v.at[:, part], out.at[:, part], out_sem.at[i])

    def march(c, carry):
        w_re, w_im, d_re, d_im = carry
        w_re = w_re + d_re
        w_im = w_im + d_im
        out_v[0, c] = w_re - turned[0, c]
        out_v[1, c] = w_im - turned[1, c]
        d_re = d_re + (rho[0, c] + inv * w_im)
        d_im = d_im + (rho[1, c] - inv * w_re)
        return w_re, w_im, d_re, d_im

    carry = (w[0], w[1], d[0], d[1])
    for i in range(chunks):
        carry = lax.fori_loop(i * chunk, (i + 1) * chunk, march, carry, unroll=4)
        store(i).start()

    @pl.when(gy > 0)
    def _():
        down.wait_send()

    @pl.when(gy < wide - 1)
    def _():
        up.wait_send()

    @pl.loop(1, count)
    def _(off):
        message(lax.rem(gx + off, count)).wait_send()

    for i in range(chunks):
        store(i).wait()


def shards(psi, potential):
    unused, cells, planes, lines = psi.shape
    count = lax.axis_size("gx")
    wide = lax.axis_size("gy")
    place, weights, coef = tables(cells, count)
    chunk = 8 if cells % 8 == 0 else cells
    chunks = cells // chunk
    block = (2, cells, planes, lines)
    return pl.pallas_call(
        functools.partial(kernel, count, wide, coef, chunk),
        out_shape=jax.ShapeDtypeStruct(block, jnp.float32),
        in_specs=[
            pl.BlockSpec(memory_space=pl.ANY),
            pl.BlockSpec(memory_space=pl.ANY),
            pl.BlockSpec(memory_space=pltpu.SMEM),
            pl.BlockSpec(memory_space=pltpu.VMEM),
        ],
        out_specs=pl.BlockSpec(memory_space=pl.ANY),
        scratch_shapes=[
            pltpu.VMEM(block, jnp.float32),
            pltpu.VMEM(block[1:], jnp.float32),
            pltpu.VMEM(block, jnp.float32),
            pltpu.VMEM(block, jnp.float32),
            pltpu.VMEM(block, jnp.float32),
            pltpu.VMEM((2, 3, planes, LANES), jnp.float32),
            pltpu.VMEM((2, 3, planes, LANES), jnp.float32),
            pltpu.VMEM((2, 2, planes, lines), jnp.float32),
            pltpu.VMEM((count, 2, planes, lines), jnp.float32),
            pltpu.SemaphoreType.DMA((2, chunks)),
            pltpu.SemaphoreType.DMA((chunks,)),
            pltpu.SemaphoreType.DMA((2,)),
            pltpu.SemaphoreType.DMA((2,)),
            pltpu.SemaphoreType.DMA((count,)),
            pltpu.SemaphoreType.DMA((count,)),
        ],
        compiler_params=pltpu.CompilerParams(collective_id=0, has_side_effects=True),
    )(psi, potential, jnp.asarray(place), jnp.asarray(weights))


def solution(mesh):
    return jax.shard_map(
        shards,
        mesh=mesh,
        in_specs=(P(None, "gx", None, "gy"), P("gx", None, "gy")),
        out_specs=P(None, "gx", None, "gy"),
        check_vma=False,
    )
```

time: 313 us -> 18.9 us (0.06)
  the two profiles are of different devices: /device:TPU:0 before, /device:TPU:1 now
where the time goes in v1:
time: 18.9 us; the launch traced here: 18.7 us
  Pallas kernels  16.4 us (87%)
  local copies, waits for them, and re-layouts  2.26 us (12%)
    pallas_call x1, Pallas kernels, shards(): pl.pallas_call(functools.partial(kernel, count, wide, coef, chunk), out_s...  16.4 us
    unnamed x1, local copies, waits for them, and re-layouts  2.26 us

profile of v1, /device:TPU:1, one launch (start us, length us, event | category | flops | bytes accessed | tf_op | source)
XLA Modules:
  0.0 18.7 jit_solution(6591706369215726068)
XLA Ops:
  0.0 16.4 %shard_map.46 = f32[2,32,16,256]{3,2,1,0:T(8,128)} custom-call(f32[2,32,16,256]{3,2,1,0:T(8,128)} %psi.1, f32[32,16,256]{2,1,0:T(8,128)} %pot.1, f32[128]{0:T(128)} %constant.4.clone.place_ref, f32[8,128]{1,0:T(8,128)} %constant.5.clone.weights), custom_call_target="tpu_custom_call" | custom-call | tf_op jit(solution)/shard_map/pallas_call | solution.py:294
  16.4 2.3 %copy.6 = f32[2,32,16,256]{3,2,1,0:T(8,128)} copy(f32[2,32,16,256]{3,2,1,0:T(8,128)} %shard_map.46) | data formatting | bytes 2097152

commit v2 on v1

--- a/solution.py
+++ b/solution.py
@@ -67,8 +67,8 @@
     return re * cosine + im * sine, im * cosine - re * sine
 
 
-def kernel(count, wide, coef, chunk, psi, pot, place_ref, weights, out, psi_v, pot_v, turned, rho,
-           out_v, edge, halo, fr, recv, in_sem, out_sem, hs_sem, hr_sem, s_sem, r_sem):
+def kernel(count, wide, coef, chunk, psi, pot, place_in, weights_in, turned, rho,
+           start, place_ref, weights, table_sem, psi_v, pot_v, edge, halo, fr, recv, in_sem, hs_sem, hr_sem, s_sem, r_sem):
     cells, planes, lines = pot_v.shape
     chunks = cells // chunk
     gx = lax.axis_index("gx")
@@ -85,6 +85,13 @@
     for i in range(chunks):
         for copy in load(i):
             copy.start()
+
+    constants = (
+        pltpu.make_async_copy(place_in, place_ref, table_sem.at[0]),
+        pltpu.make_async_copy(weights_in, weights, table_sem.at[1]),
+    )
+    for copy in constants:
+        copy.start()
 
     barrier = pltpu.get_barrier_semaphore()
 
@@ -122,30 +129,6 @@
         edge[0, which] = packed[2 * which]
         edge[1, which] = packed[2 * which + 1]
 
-    greeted = jnp.where(gy > 0, 1, 0) + jnp.where(gy < wide - 1, 1, 0)
-    pl.semaphore_wait(barrier, count - 1 + greeted)
-
-    down = pltpu.make_async_remote_copy(edge.at[0], halo.at[1], hs_sem.at[0], hr_sem.at[1],
-                                        device_id={"gy": gy - 1}, device_id_type=MESH)
-    up = pltpu.make_async_remote_copy(edge.at[1], halo.at[0], hs_sem.at[1], hr_sem.at[0],
-                                      device_id={"gy": gy + 1}, device_id_type=MESH)
-
-    @pl.when(gy > 0)
-    def _():
-        down.start()
-
-    @pl.when(gy == 0)
-    def _():
-        halo[0] = jnp.zeros(halo.shape[1:], jnp.float32)
-
-    @pl.when(gy < wide - 1)
-    def _():
-        up.start()
-
-    @pl.when(gy == wide - 1)
-    def _():
-        halo[1] = jnp.zeros(halo.shape[1:], jnp.float32)
-
     def advance(c, carry):
         e_re, e_im, q_re, q_im = carry
         t_re, t_im = turn(psi_v[0, c], psi_v[1, c], pot_v[c])
@@ -157,6 +140,32 @@
 
     zero = jnp.zeros((planes, lines), jnp.float32)
     e_re, e_im, q_re, q_im = lax.fori_loop(0, cells, advance, (zero,) * 4, unroll=2)
+
+    for copy in constants:
+        copy.wait()
+    greeted = jnp.where(gy > 0, 1, 0) + jnp.where(gy < wide - 1, 1, 0)
+    pl.semaphore_wait(barrier, count - 1 + greeted)
+
+    down = pltpu.make_async_remote_copy(edge.at[0], halo.at[1], hs_sem.at[0], hr_sem.at[1],
+                                        device_id={"gy": gy - 1}, device_id_type=MESH)
+    up = pltpu.make_async_remote_copy(edge.at[1], halo.at[0], hs_sem.at[1], hr_sem.at[0],
+                                      device_id={"gy": gy + 1}, device_id_type=MESH)
+
+    @pl.when(gy > 0)
+    def _():
+        down.start()
+
+    @pl.when(gy == 0)
+    def _():
+        halo[0] = jnp.zeros(halo.shape[1:], jnp.float32)
+
+    @pl.when(gy < wide - 1)
+    def _():
+        up.start()
+
+    @pl.when(gy == wide - 1)
+    def _():
+        halo[1] = jnp.zeros(halo.shape[1:], jnp.float32)
 
     @pl.when(gy > 0)
     def _():
@@ -248,6 +257,27 @@
     w = both(scalar(4), left, scalar(5), right)
     d = both(scalar(6), left, scalar(7), right)
 
+    for index, value in enumerate(w + d):
+        start[index] = value
+
+    @pl.when(gy > 0)
+    def _():
+        down.wait_send()
+
+    @pl.when(gy < wide - 1)
+    def _():
+        up.wait_send()
+
+    @pl.loop(1, count)
+    def _(off):
+        message(lax.rem(gx + off, count)).wait_send()
+
+
+def finish(coef, chunk, turned, rho, start, out, out_v, out_sem):
+    cells = turned.shape[1]
+    chunks = cells // chunk
+    inv = np.float32(1.0 / coef)
+
     def store(i):
         part = pl.ds(i * chunk, chunk)
         return pltpu.make_async_copy(out_v.at[:, part], out.at[:, part], out_sem.at[i])
@@ -262,23 +292,10 @@
         d_im = d_im + (rho[1, c] - inv * w_re)
         return w_re, w_im, d_re, d_im
 
-    carry = (w[0], w[1], d[0], d[1])
+    carry = (start[0], start[1], start[2], start[3])
     for i in range(chunks):
         carry = lax.fori_loop(i * chunk, (i + 1) * chunk, march, carry, unroll=4)
         store(i).start()
-
-    @pl.when(gy > 0)
-    def _():
-        down.wait_send()
-
-    @pl.when(gy < wide - 1)
-    def _():
-        up.wait_send()
-
-    @pl.loop(1, count)
-    def _(off):
-        message(lax.rem(gx + off, count)).wait_send()
-
     for i in range(chunks):
         store(i).wait()
 
@@ -291,35 +308,53 @@
     chunk = 8 if cells % 8 == 0 else cells
     chunks = cells // chunk
     block = (2, cells, planes, lines)
-    return pl.pallas_call(
+    plane = (planes, lines)
+    vmem = pl.BlockSpec(memory_space=pltpu.VMEM)
+    held = pl.pallas_call(
         functools.partial(kernel, count, wide, coef, chunk),
-        out_shape=jax.ShapeDtypeStruct(block, jnp.float32),
+        out_shape=[
+            jax.ShapeDtypeStruct(block, jnp.float32),
+            jax.ShapeDtypeStruct(block, jnp.float32),
+            jax.ShapeDtypeStruct((4,) + plane, jnp.float32),
+        ],
         in_specs=[
-            pl.BlockSpec(memory_space=pl.ANY),
-            pl.BlockSpec(memory_space=pl.ANY),
-            pl.BlockSpec(memory_space=pltpu.SMEM),
-            pl.BlockSpec(memory_space=pltpu.VMEM),
+            pl.BlockSpec(memory_space=pltpu.HBM),
+            pl.BlockSpec(memory_space=pltpu.HBM),
+            pl.BlockSpec(memory_space=pltpu.HBM),
+            pl.BlockSpec(memory_space=pltpu.HBM),
         ],
-        out_specs=pl.BlockSpec(memory_space=pl.ANY),
+        out_specs=[vmem] * 3,
         scratch_shapes=[
+            pltpu.SMEM(place.shape, jnp.float32),
+            pltpu.VMEM(weights.shape, jnp.float32),
+            pltpu.SemaphoreType.DMA((2,)),
             pltpu.VMEM(block, jnp.float32),
             pltpu.VMEM(block[1:], jnp.float32),
-            pltpu.VMEM(block, jnp.float32),
-            pltpu.VMEM(block, jnp.float32),
-            pltpu.VMEM(block, jnp.float32),
             pltpu.VMEM((2, 3, planes, LANES), jnp.float32),
             pltpu.VMEM((2, 3, planes, LANES), jnp.float32),
-            pltpu.VMEM((2, 2, planes, lines), jnp.float32),
-            pltpu.VMEM((count, 2, planes, lines), jnp.float32),
+            pltpu.VMEM((2, 2) + plane, jnp.float32),
+            pltpu.VMEM((count, 2) + plane, jnp.float32),
             pltpu.SemaphoreType.DMA((2, chunks)),
-            pltpu.SemaphoreType.DMA((chunks,)),
             pltpu.SemaphoreType.DMA((2,)),
             pltpu.SemaphoreType.DMA((2,)),
             pltpu.SemaphoreType.DMA((count,)),
             pltpu.SemaphoreType.DMA((count,)),
         ],
-        compiler_params=pltpu.CompilerParams(collective_id=0, has_side_effects=True),
+        compiler_params=pltpu.CompilerParams(
+            collective_id=0, has_side_effects=True, vmem_limit_bytes=24 * 2**20
+        ),
     )(psi, potential, jnp.asarray(place), jnp.asarray(weights))
+    return pl.pallas_call(
+        functools.partial(finish, coef, chunk),
+        out_shape=jax.ShapeDtypeStruct(block, jnp.float32),
+        in_specs=[vmem] * 3,
+        out_specs=pl.BlockSpec(memory_space=pl.ANY),
+        scratch_shapes=[
+            pltpu.VMEM(block, jnp.float32),
+            pltpu.SemaphoreType.DMA((chunks,)),
+        ],
+        compiler_params=pltpu.CompilerParams(vmem_limit_bytes=16 * 2**20),
+    )(*held)
 
 
 def solution(mesh):

time: 18.9 us -> 18.7 us (0.989)
  Pallas kernels: 16.4 us -> 14.9 us
  local copies, waits for them, and re-layouts: 2.26 us -> 3.61 us
    pallas_call x1, Pallas kernels: 16.4 us -> 13.8 us  [shards(): pl.pallas_call(functools.partial(kernel, count, wide, coef, chunk), out_s...]
    unnamed x1 -> x8, local copies, waits for them, and re-layouts: 2.26 us -> 3.61 us
    pallas_call x0 -> x1, Pallas kernels: none -> 1.05 us  [shards(): pl.pallas_call(functools.partial(finish, coef, chunk), out_shape=jax.Shap...]
where the time goes in v2:
time: 18.7 us; the launch traced here: 18.5 us
  Pallas kernels  14.9 us (80%)
  local copies, waits for them, and re-layouts  3.61 us (19%)
    pallas_call x1, Pallas kernels, shards(): pl.pallas_call(functools.partial(kernel, count, wide, coef, chunk), out_s...  13.8 us
    unnamed x8, local copies, waits for them, and re-layouts  3.61 us
    pallas_call x1, Pallas kernels, shards(): pl.pallas_call(functools.partial(finish, coef, chunk), out_shape=jax.Shap...  1.05 us

profile of v2, /device:TPU:1, one launch (start us, length us, event | category | flops | bytes accessed | tf_op | source)
XLA Modules:
  0.0 18.5 jit_solution(5854393146610913829)
XLA Ops:
  0.0 0.0 copy-start
  0.0 1.2 %copy-done = f32[2,32,16,256]{3,2,1,0:T(8,128)S(1)} copy-done((f32[2,32,16,256]{3,2,1,0:T(8,128)S(1)}, f32[2,32,16,256]{3,2,1,0:T(8,128)}, u32[]{:S(2)}) %copy-start) | copy-done | bytes 1048600
  1.2 0.0 copy-start.1
  1.2 1.0 %copy-done.1 = f32[32,16,256]{2,1,0:T(8,128)S(1)} copy-done((f32[32,16,256]{2,1,0:T(8,128)S(1)}, f32[32,16,256]{2,1,0:T(8,128)}, u32[]{:S(2)}) %copy-start.1) | copy-done | bytes 524312
  2.3 0.0 copy-start.2
  2.3 0.7 %copy-done.2 = f32[8,128]{1,0:T(8,128)S(1)} copy-done((f32[8,128]{1,0:T(8,128)S(1)}, f32[8,128]{1,0:T(8,128)}, u32[]{:S(2)}) %copy-start.2) | copy-done | bytes 4120
  3.0 0.0 copy-start.3
  3.0 0.7 %copy-done.3 = f32[128]{0:T(128)S(1)} copy-done((f32[128]{0:T(128)S(1)}, f32[128]{0:T(128)}, u32[]{:S(2)}) %copy-start.3) | copy-done | bytes 536
  3.6 13.8 %shard_map.46 = (f32[2,32,16,256]{3,2,1,0:T(8,128)S(1)}, f32[2,32,16,256]{3,2,1,0:T(8,128)S(1)}, f32[4,16,256]{2,1,0:T(8,128)S(1)}) custom-call(f32[2,32,16,256]{3,2,1,0:T(8,128)S(1)} %copy-done, f32[32,16,256]{2,1,0:T(8,128)S(1)} %copy-done.1, f32[128]{0:T(128)S(1)} %copy-done.3, f32[8,128]{1,0:T(8,128)S(1)} %copy-done.2), custom_call_target="tpu_custom_call" | custom-call | tf_op jit(solution)/shard_map/pallas_call | solution.py:313
  17.4 1.1 %shard_map.47 = f32[2,32,16,256]{3,2,1,0:T(8,128)} custom-call(f32[2,32,16,256]{3,2,1,0:T(8,128)S(1)} %get-tuple-element.8.turned, f32[2,32,16,256]{3,2,1,0:T(8,128)S(1)} %get-tuple-element.9.rho, f32[4,16,256]{2,1,0:T(8,128)S(1)} %get-tuple-element.10.start), custom_call_target="tpu_custom_call" | custom-call | tf_op jit(solution)/shard_map/pallas_call | solution.py:347
Async XLA Ops:
  0.0 1.2 %copy-start = (f32[2,32,16,256]{3,2,1,0:T(8,128)S(1)}, f32[2,32,16,256]{3,2,1,0:T(8,128)}, u32[]{:S(2)}) copy-start(f32[2,32,16,256]{3,2,1,0:T(8,128)} %psi.1) | copy-start | bytes 3145732
  1.2 1.0 %copy-start.1 = (f32[32,16,256]{2,1,0:T(8,128)S(1)}, f32[32,16,256]{2,1,0:T(8,128)}, u32[]{:S(2)}) copy-start(f32[32,16,256]{2,1,0:T(8,128)} %pot.1) | copy-start | bytes 1572868
  2.3 0.7 %copy-start.2 = (f32[8,128]{1,0:T(8,128)S(1)}, f32[8,128]{1,0:T(8,128)}, u32[]{:S(2)}) copy-start(f32[8,128]{1,0:T(8,128)} %constant.5.clone.weights_in) | copy-start | bytes 12292
  3.0 0.7 %copy-start.3 = (f32[128]{0:T(128)S(1)}, f32[128]{0:T(128)}, u32[]{:S(2)}) copy-start(f32[128]{0:T(128)} %constant.4.clone.place_in) | copy-start | bytes 1540

commit v3 on v2

--- a/solution.py
+++ b/solution.py
@@ -343,7 +343,8 @@
         compiler_params=pltpu.CompilerParams(
             collective_id=0, has_side_effects=True, vmem_limit_bytes=24 * 2**20
         ),
-    )(psi, potential, jnp.asarray(place), jnp.asarray(weights))
+    )(*(pltpu.with_memory_space_constraint(x, pltpu.HBM) for x in
+        (psi, potential, jnp.asarray(place), jnp.asarray(weights))))
     return pl.pallas_call(
         functools.partial(finish, coef, chunk),
         out_shape=jax.ShapeDtypeStruct(block, jnp.float32),

time: 18.7 us -> 15.5 us (0.83)
  local copies, waits for them, and re-layouts: 3.61 us -> 0 us
  Pallas kernels: 14.9 us -> 15.3 us
    unnamed x8 -> x0, local copies, waits for them, and re-layouts: 3.61 us -> none
    pallas_call x1, Pallas kernels: 13.8 us -> 14.3 us  [shards(): pl.pallas_call(functools.partial(kernel, count, wide, coef, chunk), out_s...]
where the time goes in v3:
time: 15.5 us; the launch traced here: 15.4 us
  Pallas kernels  15.3 us (99%)
    pallas_call x1, Pallas kernels, shards(): pl.pallas_call(functools.partial(kernel, count, wide, coef, chunk), out_s...  14.3 us
    pallas_call x1, Pallas kernels, shards(): pl.pallas_call(functools.partial(finish, coef, chunk), out_shape=jax.Shap...  1.05 us

profile of v3, /device:TPU:1, one launch (start us, length us, event | category | flops | bytes accessed | tf_op | source)
XLA Modules:
  0.0 15.4 jit_solution(3946838714269629187)
XLA Ops:
  0.0 14.3 %shard_map.46 = (f32[2,32,16,256]{3,2,1,0:T(8,128)S(1)}, f32[2,32,16,256]{3,2,1,0:T(8,128)S(1)}, f32[4,16,256]{2,1,0:T(8,128)S(1)}) custom-call(f32[2,32,16,256]{3,2,1,0:T(8,128)} %psi.1, f32[32,16,256]{2,1,0:T(8,128)} %pot.1, f32[128]{0:T(128)} %constant.4.clone.place_in, f32[8,128]{1,0:T(8,128)} %constant.5.clone.weights_in), custom_call_target="tpu_custom_call" | custom-call | tf_op jit(solution)/shard_map/pallas_call | solution.py:313
  14.3 1.1 %shard_map.47 = f32[2,32,16,256]{3,2,1,0:T(8,128)} custom-call(f32[2,32,16,256]{3,2,1,0:T(8,128)S(1)} %get-tuple-element.8.turned, f32[2,32,16,256]{3,2,1,0:T(8,128)S(1)} %get-tuple-element.9.rho, f32[4,16,256]{2,1,0:T(8,128)S(1)} %get-tuple-element.10.start), custom_call_target="tpu_custom_call" | custom-call | tf_op jit(solution)/shard_map/pallas_call | solution.py:348

commit v4 on v3

--- a/solution.py
+++ b/solution.py
@@ -68,7 +68,8 @@
 
 
 def kernel(count, wide, coef, chunk, psi, pot, place_in, weights_in, turned, rho,
-           start, place_ref, weights, table_sem, psi_v, pot_v, edge, halo, fr, recv, in_sem, hs_sem, hr_sem, s_sem, r_sem):
+           start, place_ref, weights, table_sem, psi_v, pot_v, edge, halo, fr, recv, in_sem, hs_sem, hr_sem, s_sem, r_sem,
+           fx, fx_recv, fs_sem, fr_sem):
     cells, planes, lines = pot_v.shape
     chunks = cells // chunk
     gx = lax.axis_index("gx")
@@ -143,6 +144,41 @@
 
     for copy in constants:
         copy.wait()
+
+    col = lax.broadcasted_iota(jnp.int32, (planes, lines), 1)
+    row = lax.broadcasted_iota(jnp.int32, (planes, lines), 0)
+    at_first, at_last = col == 0, col == lines - 1
+    at_bottom, at_top = row == 0, row == planes - 1
+
+    def lap(x, first, last):
+        left = jnp.where(at_first, first, pltpu.roll(x, 1, 1))
+        right = jnp.where(at_last, last, pltpu.roll(x, lines - 1, 1))
+        below = jnp.where(at_bottom, 0.0, pltpu.roll(x, 1, 0))
+        above = jnp.where(at_top, 0.0, pltpu.roll(x, planes - 1, 0))
+        return ((left + right) + (below + above)) - 4.0 * x
+
+    def stencil(re, im, first, last):
+        lap_re = lap(re, first[0], last[0])
+        lap_im = lap(im, first[1], last[1])
+        return 2.0 * re - RYZ * lap_im, 2.0 * im + RYZ * lap_re
+
+    e_re, e_im = stencil(e_re, e_im, (0.0, 0.0), (0.0, 0.0))
+    q_re, q_im = stencil(q_re, q_im, (0.0, 0.0), (0.0, 0.0))
+
+    def scalar(index):
+        return place_ref[gx * 16 + 2 * index], place_ref[gx * 16 + 2 * index + 1]
+
+    def both(a, x, b, y):
+        return (
+            (a[0] * x[0] - a[1] * x[1]) + (b[0] * y[0] - b[1] * y[1]),
+            (a[0] * x[1] + a[1] * x[0]) + (b[0] * y[1] + b[1] * y[0]),
+        )
+
+    for which in range(2):
+        value = both(scalar(2 * which), (q_re, q_im), scalar(2 * which + 1), (e_re, e_im))
+        fr[which, 0] = value[0]
+        fr[which, 1] = value[1]
+
     greeted = jnp.where(gy > 0, 1, 0) + jnp.where(gy < wide - 1, 1, 0)
     pl.semaphore_wait(barrier, count - 1 + greeted)
 
@@ -166,6 +202,15 @@
     @pl.when(gy == wide - 1)
     def _():
         halo[1] = jnp.zeros(halo.shape[1:], jnp.float32)
+
+    def message(peer):
+        return pltpu.make_async_remote_copy(
+            fr.at[jnp.where(peer < gx, 1, 0)], recv.at[gx], s_sem.at[peer], r_sem.at[gx],
+            device_id={"gx": peer}, device_id_type=MESH)
+
+    @pl.loop(1, count)
+    def _(off):
+        message(lax.rem(gx + off, count)).start()
 
     @pl.when(gy > 0)
     def _():
@@ -188,48 +233,26 @@
             (total(g_re * h_re - g_im * h_im), total(g_re * h_im + g_im * h_re)),
         ))
 
-    col = lax.broadcasted_iota(jnp.int32, (planes, lines), 1)
-    row = lax.broadcasted_iota(jnp.int32, (planes, lines), 0)
-    at_first, at_last = col == 0, col == lines - 1
-    at_bottom, at_top = row == 0, row == planes - 1
-
-    def lap(x, first, last):
-        left = jnp.where(at_first, first, pltpu.roll(x, 1, 1))
-        right = jnp.where(at_last, last, pltpu.roll(x, lines - 1, 1))
-        below = jnp.where(at_bottom, 0.0, pltpu.roll(x, 1, 0))
-        above = jnp.where(at_top, 0.0, pltpu.roll(x, planes - 1, 0))
-        return ((left + right) + (below + above)) - 4.0 * x
-
-    def stencil(re, im, first, last):
-        lap_re = lap(re, first[0], last[0])
-        lap_im = lap(im, first[1], last[1])
-        return 2.0 * re - RYZ * lap_im, 2.0 * im + RYZ * lap_re
-
-    e_re, e_im = stencil(e_re, e_im, sums[0][0], sums[1][0])
-    q_re, q_im = stencil(q_re, q_im, sums[0][1], sums[1][1])
-
-    def scalar(index):
-        return place_ref[gx * 16 + 2 * index], place_ref[gx * 16 + 2 * index + 1]
-
-    def both(a, x, b, y):
-        return (
-            (a[0] * x[0] - a[1] * x[1]) + (b[0] * y[0] - b[1] * y[1]),
-            (a[0] * x[1] + a[1] * x[0]) + (b[0] * y[1] + b[1] * y[0]),
-        )
+    def turned_sum(value):
+        return -2.0 * value[1], 2.0 * value[0]
 
     for which in range(2):
-        value = both(scalar(2 * which), (q_re, q_im), scalar(2 * which + 1), (e_re, e_im))
-        fr[which, 0] = value[0]
-        fr[which, 1] = value[1]
-
-    def message(peer):
+        tile = zero_edge
+        for side in range(2):
+            value = both(scalar(2 * which), turned_sum(sums[side][1]),
+                         scalar(2 * which + 1), turned_sum(sums[side][0]))
+            tile = jnp.where(lane == 2 * side, value[0], tile)
+            tile = jnp.where(lane == 2 * side + 1, value[1], tile)
+        fx[which] = tile
+
+    def fixing(peer):
         return pltpu.make_async_remote_copy(
-            fr.at[jnp.where(peer < gx, 1, 0)], recv.at[gx], s_sem.at[peer], r_sem.at[gx],
+            fx.at[jnp.where(peer < gx, 1, 0)], fx_recv.at[gx], fs_sem.at[peer], fr_sem.at[gx],
             device_id={"gx": peer}, device_id_type=MESH)
 
     @pl.loop(1, count)
     def _(off):
-        message(lax.rem(gx + off, count)).start()
+        fixing(lax.rem(gx + off, count)).start()
 
     h_all = (sides[0][0], sides[0][1], sides[1][0], sides[1][1])
 
@@ -248,12 +271,30 @@
             fr.at[0], recv.at[k], s_sem.at[k], r_sem.at[k],
             device_id={"gx": k}, device_id_type=MESH)
 
+    def fix_arrival(k):
+        return pltpu.make_async_remote_copy(
+            fx.at[0], fx_recv.at[k], fs_sem.at[k], fr_sem.at[k],
+            device_id={"gx": k}, device_id_type=MESH)
+
     def take(k, acc):
         arrival(k).wait_recv()
         return acc[0] + recv[k, 0], acc[1] + recv[k, 1]
 
+    def take_fix(k, acc):
+        fix_arrival(k).wait_recv()
+        return acc + fx_recv[k]
+
+    def spread(value, tile):
+        return tuple(
+            value[part]
+            + jnp.where(at_first, tile[:, part : part + 1], 0.0)
+            + jnp.where(at_last, tile[:, 2 + part : 3 + part], 0.0)
+            for part in range(2))
+
     left = lax.fori_loop(0, gx, take, (zero, zero))
     right = lax.fori_loop(gx + 1, count, take, (fr[1, 0], fr[1, 1]))
+    left = spread(left, lax.fori_loop(0, gx, take_fix, zero_edge))
+    right = spread(right, lax.fori_loop(gx + 1, count, take_fix, fx[1]))
     w = both(scalar(4), left, scalar(5), right)
     d = both(scalar(6), left, scalar(7), right)
 
@@ -271,6 +312,7 @@
     @pl.loop(1, count)
     def _(off):
         message(lax.rem(gx + off, count)).wait_send()
+        fixing(lax.rem(gx + off, count)).wait_send()
 
 
 def finish(coef, chunk, turned, rho, start, out, out_v, out_sem):
@@ -339,6 +381,10 @@
             pltpu.SemaphoreType.DMA((2,)),
             pltpu.SemaphoreType.DMA((count,)),
             pltpu.SemaphoreType.DMA((count,)),
+            pltpu.VMEM((2, planes, LANES), jnp.float32),
+            pltpu.VMEM((count, planes, LANES), jnp.float32),
+            pltpu.SemaphoreType.DMA((count,)),
+            pltpu.SemaphoreType.DMA((count,)),
         ],
         compiler_params=pltpu.CompilerParams(
             collective_id=0, has_side_effects=True, vmem_limit_bytes=24 * 2**20

time: 15.5 us -> 18.1 us (1.17)
  the two profiles are of different devices: /device:TPU:1 before, /device:TPU:0 now
where the time goes in v4:
time: 18.1 us; the launch traced here: 18 us
  Pallas kernels  17.9 us (99%)
    pallas_call x1, Pallas kernels, shards(): pl.pallas_call(functools.partial(kernel, count, wide, coef, chunk), out_s...  16.9 us
    pallas_call x1, Pallas kernels, shards(): pl.pallas_call(functools.partial(finish, coef, chunk), out_shape=jax.Shap...  1.05 us

profile of v4, /device:TPU:0, one launch (start us, length us, event | category | flops | bytes accessed | tf_op | source)
XLA Modules:
  0.0 18.0 jit_solution(10125565778689204208)
XLA Ops:
  0.0 16.9 %shard_map.46 = (f32[2,32,16,256]{3,2,1,0:T(8,128)S(1)}, f32[2,32,16,256]{3,2,1,0:T(8,128)S(1)}, f32[4,16,256]{2,1,0:T(8,128)S(1)}) custom-call(f32[2,32,16,256]{3,2,1,0:T(8,128)} %psi.1, f32[32,16,256]{2,1,0:T(8,128)} %pot.1, f32[128]{0:T(128)} %constant.4.clone.place_in, f32[8,128]{1,0:T(8,128)} %constant.5.clone.weights_in), custom_call_target="tpu_custom_call" | custom-call | tf_op jit(solution)/shard_map/pallas_call | solution.py:355
  16.9 1.1 %shard_map.47 = f32[2,32,16,256]{3,2,1,0:T(8,128)} custom-call(f32[2,32,16,256]{3,2,1,0:T(8,128)S(1)} %get-tuple-element.8.turned, f32[2,32,16,256]{3,2,1,0:T(8,128)S(1)} %get-tuple-element.9.rho, f32[4,16,256]{2,1,0:T(8,128)S(1)} %get-tuple-element.10.start), custom_call_target="tpu_custom_call" | custom-call | tf_op jit(solution)/shard_map/pallas_call | solution.py:394
